TPU v7x, 128 devices: a whole 4x4x4 slice. The times are simulated.
128 devices in a mesh: seq: 32 (over x, z_lo, y), head: 2 (over core), dp: 2 (over z_hi).
Axes of the slice: x: 4, y: 4, z: 4 (z_hi: 2, z_lo: 2; z = z_hi * 2 + z_lo), core: 2. Of those that a mesh axis runs over, the one named last changes fastest.
Arguments:
- queries: bfloat16 [16384, 2048], P(('dp', 'seq'), 'head'), parts along dimension 0, may hold values from -32 to 32
- keys: bfloat16 [16384, 2048], P(('dp', 'seq'), 'head'), parts along dimension 0, may hold values from -32 to 32
- values: bfloat16 [16384, 2048], P(('dp', 'seq'), 'head'), parts along dimension 0, may hold values from -6 to 6
- out_grad: bfloat16 [16384, 4096], P(('dp', 'seq')), parts along dimension 0, may hold values from -6 to 6
- proj_weight: bfloat16 [4096, 2048], P(None, 'head'), may hold values from -0.09375 to 0.09375
- layout: int32 [64, 12], replicated, may hold values from -1 to 63, as said below
Outputs:
- query_grad: bfloat16 [16384, 2048], P(('dp', 'seq'), 'head'), parts along dimension 0
- key_grad: bfloat16 [16384, 2048], P(('dp', 'seq'), 'head'), parts along dimension 0
- value_grad: bfloat16 [16384, 2048], P(('dp', 'seq'), 'head'), parts along dimension 0
- proj_grad: float32 [8192, 2048], P(('dp', 'seq'), 'head'), parts along dimension 0
There are 2 independent parts, one for each index of `dp`. A program takes and returns all parts, laid end to end along the dimension named above; an argument that names none is the same for every part. Nothing has to cross between parts.
Inputs may be any that keep to these rules, and one draw needn't show every extreme that they name: `layout`: row i lists, in increasing order, some of the blocks j < i - 7 whose remainder modulo 16 equals one offset, below 8 and shared by all rows (the last row lists all of them), then the blocks max(0, i - w + 1) to i for a window w of its own between 1 and 8, and ends with -1 in the unused entries; a row whose block follows a block of that remainder has w = 8.
All inputs are finite; a program needn't handle non-finite values.
Results may differ from a plain program's by a relative error of at most 0.03.
Values may be sent and summed in bfloat16 or wider, within the bound.
A program may use at most 192 MiB of HBM per device.

v0:
```python
import jax
import jax.numpy as jnp
from jax import lax
from jax.sharding import PartitionSpec as P

HD = 128
BLK = 128
LOCAL = 8
STRIDE = 16


def passed_along(block, axis, distance):
    devices = range(lax.axis_size(axis))
    route = [(i - distance, i) for i in devices if i - distance in devices]
    return lax.ppermute(block, axis, route)


def listed(table_rows, block_ids):
    hit = jnp.any(table_rows[:, None, :] == block_ids[:, :, None], axis=2)
    return hit & (block_ids >= 0)


def local(queries, keys, values, out_grad, proj_weight, layout):
    tok_dev = queries.shape[0]
    width = queries.shape[1]
    heads_here = width // HD
    blocks_dev = tok_dev // BLK
    block_count = layout.shape[0]
    summary_count = block_count // STRIDE
    score_scale = HD ** (-0.5)
    me = lax.axis_index("seq")
    first_block = me * blocks_dev
    offset_block = layout[block_count - 1, 0] % STRIDE
    reach_back = (LOCAL - 2) // blocks_dev + 1
    span_blocks = [
        min(blocks_dev, LOCAL - 1 - hop_index * blocks_dev) for hop_index in range(reach_back)
    ]
    back_blocks = sum(span_blocks)
    pool_blocks = back_blocks + blocks_dev
    attn_grad = jnp.dot(out_grad, proj_weight, preferred_element_type=jnp.float32).astype(
        jnp.bfloat16
    )
    kv = jnp.concatenate([keys, values], axis=1)
    near = []
    for distance in range(reach_back, 0, -1):
        rows_needed = span_blocks[distance - 1] * BLK
        near.append(passed_along(kv[tok_dev - rows_needed :], "seq", distance))
    pool_kv = jnp.concatenate(near + [kv], axis=0)
    far_ids = jnp.arange(summary_count, dtype=jnp.int32) * STRIDE + offset_block
    far_owner = far_ids // blocks_dev
    far_local = far_ids % blocks_dev
    kv_blocks = kv.reshape(blocks_dev, BLK, 2 * width)
    far_mine = jnp.where(
        (far_owner == me)[:, None, None],
        jnp.take(kv_blocks, far_local, axis=0),
        jnp.zeros_like(kv_blocks[:1]),
    ).reshape(summary_count * BLK, 2 * width)
    far_part = lax.psum_scatter(far_mine, "seq", scatter_dimension=0, tiled=True)
    far_kv = lax.all_gather(far_part, "seq", axis=0, tiled=True)
    all_kv = jnp.concatenate([pool_kv, far_kv], axis=0)
    key_rows = all_kv[:, :width].reshape(-1, heads_here, HD)
    value_rows = all_kv[:, width:].reshape(-1, heads_here, HD)
    query_rows = queries.reshape(tok_dev, heads_here, HD)
    grad_rows = attn_grad.reshape(tok_dev, heads_here, HD)
    own_ids = first_block + jnp.arange(blocks_dev, dtype=jnp.int32)
    table_rows = lax.dynamic_slice_in_dim(layout, first_block, blocks_dev, 0)
    pool_ids = first_block - back_blocks + jnp.arange(pool_blocks, dtype=jnp.int32)
    pool_ids_b = jnp.broadcast_to(pool_ids[None, :], (blocks_dev, pool_blocks))
    plain = (pool_ids_b % STRIDE != offset_block) | (pool_ids_b == own_ids[:, None])
    pool_ok = listed(table_rows, pool_ids_b) & plain
    far_ids_b = jnp.broadcast_to(far_ids[None, :], (blocks_dev, summary_count))
    far_ok = listed(table_rows, far_ids_b) & (far_ids_b < own_ids[:, None])
    block_ok = jnp.concatenate([pool_ok, far_ok], axis=1)
    token_ok = jnp.repeat(jnp.repeat(block_ok, BLK, axis=0), BLK, axis=1)
    query_pos = jnp.arange(tok_dev, dtype=jnp.int32)
    pool_pos = jnp.arange(pool_blocks * BLK, dtype=jnp.int32) - back_blocks * BLK
    causal = jnp.concatenate(
        [
            pool_pos[None, :] <= query_pos[:, None],
            jnp.ones((tok_dev, summary_count * BLK), jnp.bool_),
        ],
        axis=1,
    )
    allowed = token_ok & causal
    scores = (
        jnp.einsum("qhd,khd->hqk", query_rows, key_rows, preferred_element_type=jnp.float32)
        * score_scale
    )
    scores = jnp.where(allowed[None], scores, -jnp.inf)
    row_top = jnp.max(scores, axis=-1, keepdims=True)
    log_total = row_top + jnp.log(jnp.sum(jnp.exp(scores - row_top), axis=-1, keepdims=True))
    probs = jnp.exp(scores - log_total)
    probs_low = probs.astype(jnp.bfloat16)
    attn_out = jnp.einsum(
        "hqk,khd->qhd", probs_low, value_rows, preferred_element_type=jnp.float32
    ).astype(jnp.bfloat16)
    delta = jnp.transpose(
        jnp.sum(attn_out.astype(jnp.float32) * grad_rows.astype(jnp.float32), axis=-1)
    )[..., None]
    dprobs = jnp.einsum("qhd,khd->hqk", grad_rows, value_rows, preferred_element_type=jnp.float32)
    dscores = (score_scale * probs * (dprobs - delta)).astype(jnp.bfloat16)
    query_grad = jnp.einsum(
        "hqk,khd->qhd", dscores, key_rows, preferred_element_type=jnp.float32
    ).astype(jnp.bfloat16)
    key_part = jnp.einsum("hqk,qhd->khd", dscores, query_rows, preferred_element_type=jnp.float32)
    value_part = jnp.einsum(
        "hqk,qhd->khd", probs_low, grad_rows, preferred_element_type=jnp.float32
    )
    grad_kv = jnp.concatenate([key_part.reshape(-1, width), value_part.reshape(-1, width)], axis=1)
    far_grad = grad_kv[pool_blocks * BLK :]
    far_sum = lax.all_gather(
        lax.psum_scatter(far_grad, "seq", scatter_dimension=0, tiled=True),
        "seq",
        axis=0,
        tiled=True,
    ).reshape(summary_count, BLK, 2 * width)
    is_summary = own_ids % STRIDE == offset_block
    summary_slot = jnp.minimum(own_ids // STRIDE, summary_count - 1)
    far_add = jnp.where(is_summary[:, None, None], jnp.take(far_sum, summary_slot, axis=0), 0.0)
    own_grad = grad_kv[back_blocks * BLK : pool_blocks * BLK]
    pool_start = 0
    for distance in range(reach_back, 0, -1):
        rows_needed = span_blocks[distance - 1] * BLK
        back = passed_along(grad_kv[pool_start : pool_start + rows_needed], "seq", -distance)
        own_grad = own_grad.at[tok_dev - rows_needed :].add(back)
        pool_start = pool_start + rows_needed
    total = own_grad.reshape(blocks_dev, BLK, 2 * width) + far_add
    total = total.reshape(tok_dev, 2 * width).astype(jnp.bfloat16)
    proj_grad = lax.psum_scatter(
        lax.dot_general(
            out_grad,
            attn_out.reshape(tok_dev, width),
            (((0,), (0,)), ((), ())),
            preferred_element_type=jnp.float32,
        ),
        "seq",
        scatter_dimension=0,
        tiled=True,
    )
    return (query_grad.reshape(tok_dev, width), total[:, :width], total[:, width:], proj_grad)


def solution(mesh):
    return jax.shard_map(
        local,
        mesh=mesh,
        in_specs=(
            P(("dp", "seq"), "head"),
            P(("dp", "seq"), "head"),
            P(("dp", "seq"), "head"),
            P(("dp", "seq"), None),
            P(None, "head"),
            P(),
        ),
        out_specs=(
            P(("dp", "seq"), "head"),
            P(("dp", "seq"), "head"),
            P(("dp", "seq"), "head"),
            P(("dp", "seq"), "head"),
        ),
        check_vma=False,
    )
```

profile of v0, /device:TPU:0, one launch (start us, length us, event | category | flops | bytes accessed | tf_op | source)
XLA Modules:
  0.0 1129.2 jit_solution(14929468038700556082)
XLA Ops:
  30.0 6.1 collective-permute-start.1
  36.1 4.9 collective-permute-start.2
  46.8 179.5 %reduce-scatter.10.cloned.1.call-done = bf16[16,2048]{1,0:T(8,128)(2,1)} async-done(((bf16[512,2048]{1,0:T(8,128)(2,1)}), bf16[16,2048]{1,0:T(8,128)(2,1)}) %reduce-scatter.10.cloned.1.call-update) | async-done | bytes 65552 | tf_op jit(solution)/shard_map/reduce_scatter | solution.py:58
  227.0 6.5 convolution_convert_fusion.2
  249.2 128.6 %all-gather.3.cloned.1.call-done = bf16[512,2048]{1,0:T(8,128)(2,1)} async-done(((bf16[16,2048]{1,0:T(8,128)(2,1)}), bf16[512,2048]{1,0:T(8,128)(2,1)}) %all-gather.3.cloned.1.call-update) | async-done | bytes 2097168 | tf_op jit(solution)/shard_map/all_gather | solution.py:59
  384.8 5.3 fusion.23
  390.0 7.5 fusion.1
  397.5 7.8 exponential_reduce_fusion
  405.4 10.4 multiply_reduce_fusion
  415.8 5.8 fusion.20
  421.6 10.1 multiply_convert_fusion
  431.8 7.7 copy.117
  439.5 7.9 fusion.25
  447.3 7.7 copy.116
  455.0 4.7 pad_maximum_fusion
  459.8 168.7 %reduce-scatter.6.cloned.1.call-done = f32[16,2048]{1,0:T(8,128)} async-done(((f32[512,2048]{1,0:T(8,128)}), f32[16,2048]{1,0:T(8,128)}) %reduce-scatter.6.cloned.1.call-update) | async-done | bytes 131088 | tf_op jit(solution)/shard_map/reduce_scatter | solution.py:112
  628.6 8.1 convolution_bitcast_fusion
  636.7 6.1 fusion.4
  650.6 4.1 convolution_convert_fusion
  655.7 18.4 %collective-permute-done.4 = f32[128,2048]{1,0:T(8,128)} collective-permute-done((f32[128,2048]{1,0:T(8,128)}, f32[128,2048]{1,0:T(8,128)}, u32[]{:S(2)}, u32[]{:S(2)}) %collective-permute-start.4) | collective-permute-done | bytes 1048608 | tf_op jit(solution)/shard_map/ppermute | solution.py:15
  676.8 218.7 %all-gather.5.cloned.1.call-done = f32[512,2048]{1,0:T(8,128)} async-done(((f32[16,2048]{1,0:T(8,128)}), f32[512,2048]{1,0:T(8,128)}) %all-gather.5.cloned.1.call-update) | async-done | bytes 4194320 | tf_op jit(solution)/shard_map/all_gather | solution.py:111
  895.5 4.2 gather_fusion.1
  899.7 4.6 fusion.8
  905.4 215.2 %reduce-scatter.8.cloned.1.call-done = f32[128,1024]{0,1:T(8,128)} async-done(((f32[4096,1024]{0,1:T(8,128)}), f32[128,1024]{0,1:T(8,128)}) %reduce-scatter.8.cloned.1.call-update) | async-done | bytes 524304 | tf_op jit(solution)/shard_map/reduce_scatter | solution.py:129
  (113 shorter events, 64.6 us)
Async XLA Ops:
  7.2 219.9 %copy-start = (bf16[256,4096]{1,0:T(8,128)(2,1)S(1)}, bf16[256,4096]{1,0:T(8,128)(2,1)}, u32[]{:S(2)}) copy-start(bf16[256,4096]{1,0:T(8,128)(2,1)} %param.23) | copy-start | bytes 6291460
  7.2 219.1 %reduce-scatter.10.cloned.1.call-start = ((), (), s32[]{:S(2)}) async-start(), calls=%async_computation.7 | async-start | bytes 2162688 | tf_op jit(solution)/shard_map/reduce_scatter | solution.py:58
  18.7 25.1 %copy-start.4 = (bf16[256,1024]{0,1:T(8,128)(2,1)S(1)}, bf16[256,1024]{0,1:T(8,128)(2,1)}, u32[]{:S(2)}) copy-start(bf16[256,1024]{0,1:T(8,128)(2,1)} %copy-done.3) | copy-start | bytes 1572868
  18.7 25.1 %copy-start.6 = (bf16[256,1024]{0,1:T(8,128)(2,1)S(1)}, bf16[256,1024]{0,1:T(8,128)(2,1)}, u32[]{:S(2)}) copy-start(bf16[256,1024]{0,1:T(8,128)(2,1)} %copy-done.5) | copy-start | bytes 1572868
  22.7 24.0 %copy-start.12 = (s32[64,12]{0,1:T(8,128)S(1)}, s32[64,12]{0,1:T(8,128)}, u32[]{:S(2)}) copy-start(s32[64,12]{0,1:T(8,128)} %param.25) | copy-start | bytes 9220
  30.0 347.8 %all-gather.3.cloned.1.call-start = ((), (), s32[]{:S(2)}) async-start(), calls=%async_computation.3 | async-start | bytes 2162688 | tf_op jit(solution)/shard_map/all_gather | solution.py:59
  30.0 211.0 %collective-permute-start.1 = (bf16[256,2048]{0,1:T(8,128)(2,1)}, bf16[256,2048]{0,1:T(8,128)(2,1)}, u32[]{:S(2)}, u32[]{:S(2)}) collective-permute-start(bf16[256,2048]{0,1:T(8,128)(2,1)} %pad_maximum_fusion.1), channel_id=1, source_target_pairs={{0,12},{4,16},{8,20},{12,24},{16,28},{20,32},{24,36},{28,40},{32,4... | collective-permute-start | bytes 3145736 | tf_op jit(solution)/shard_map/ppermute | solution.py:15
  36.1 207.3 %collective-permute-start.2 = (bf16[256,2048]{0,1:T(8,128)(2,1)}, bf16[256,2048]{0,1:T(8,128)(2,1)}, u32[]{:S(2)}, u32[]{:S(2)}) collective-permute-start(bf16[256,2048]{0,1:T(8,128)(2,1)} %pad_maximum_fusion.1), channel_id=1, source_target_pairs={{0,8},{4,12},{8,16},{12,20},{16,24},{20,28},{24,32},{28,36},{32,40... | collective-permute-start | bytes 3145736 | tf_op jit(solution)/shard_map/ppermute | solution.py:15
  41.0 204.8 %collective-permute-start.3 = (bf16[256,2048]{0,1:T(8,128)(2,1)}, bf16[256,2048]{0,1:T(8,128)(2,1)}, u32[]{:S(2)}, u32[]{:S(2)}) collective-permute-start(bf16[256,2048]{0,1:T(8,128)(2,1)} %pad_maximum_fusion.1), channel_id=1, source_target_pairs={{0,4},{4,8},{8,12},{12,16},{16,20},{20,24},{24,28},{28,32},{32,36}... | collective-permute-start | bytes 3145736 | tf_op jit(solution)/shard_map/ppermute | solution.py:15
  44.6 194.5 %collective-permute-start = (bf16[128,2048]{0,1:T(8,128)(2,1)}, bf16[128,2048]{0,1:T(8,128)(2,1)}, u32[]{:S(2)}, u32[]{:S(2)}) collective-permute-start(bf16[128,2048]{0,1:T(8,128)(2,1)} %fusion.13), channel_id=1, source_target_pairs={{0,16},{4,20},{8,24},{12,28},{16,32},{20,36},{24,40},{28,44},{32,4... | collective-permute-start | bytes 1572872 | tf_op jit(solution)/shard_map/ppermute | solution.py:15
  226.3 402.2 %reduce-scatter.6.cloned.1.call-start = ((), (), s32[]{:S(2)}) async-start(), calls=%async_computation.4 | async-start | bytes 4325376 | tf_op jit(solution)/shard_map/reduce_scatter | solution.py:112
  397.5 18.2 %slice-start = ((s8[13631488]{0:T(1024)(128)(4,1)}), s8[4194304]{0:T(1024)(128)(4,1)S(1)}, s32[]{:S(2)}) async-start(s8[13631488]{0:T(1024)(128)(4,1)} %bitcast.82), calls=%async_computation.8 | async-start | bytes 8388608
  397.5 18.2 %slice-start.1 = ((s8[13631488]{0:T(1024)(128)(4,1)}), s8[1048576]{0:T(1024)(128)(4,1)S(1)}, s32[]{:S(2)}) async-start(s8[13631488]{0:T(1024)(128)(4,1)} %bitcast.82), calls=%async_computation.9 | async-start | bytes 2097152
  405.3 10.4 slice-start.2
  405.3 10.4 slice-start.3
  405.3 10.4 copy-start.10
  431.8 7.7 copy-start.9
  455.0 173.6 %copy-start.11 = (bf16[8,128,256]{2,1,0:T(8,128)(2,1)S(1)}, bf16[8,128,256]{2,1,0:T(8,128)(2,1)}, u32[]{:S(2)}) copy-start(bf16[8,128,256]{2,1,0:T(8,128)(2,1)} %get-tuple-element.107) | copy-start | bytes 1572868
  459.8 435.7 %all-gather.5.cloned.1.call-start = ((), (), s32[]{:S(2)}) async-start(), calls=%async_computation.5 | async-start | bytes 4325376 | tf_op jit(solution)/shard_map/all_gather | solution.py:111
  628.5 492.1 %reduce-scatter.8.cloned.1.call-start = ((), (), s32[]{:S(2)}) async-start(), calls=%async_computation.6 | async-start | bytes 17301504 | tf_op jit(solution)/shard_map/reduce_scatter | solution.py:129
  642.8 256.9 %collective-permute-start.7 = (f32[256,2048]{1,0:T(8,128)}, f32[256,2048]{1,0:T(8,128)}, u32[]{:S(2)}, u32[]{:S(2)}) collective-permute-start(f32[256,2048]{1,0:T(8,128)} %get-tuple-element.99), channel_id=1, source_target_pairs={{4,0},{8,4},{12,8},{16,12},{20,16},{24,20},{28,24},{32,28},{36,32}... | collective-permute-start | bytes 6291464 | tf_op jit(solution)/shard_map/ppermute | solution.py:15
  644.1 255.6 %collective-permute-start.6 = (f32[256,2048]{1,0:T(8,128)}, f32[256,2048]{1,0:T(8,128)}, u32[]{:S(2)}, u32[]{:S(2)}) collective-permute-start(f32[256,2048]{1,0:T(8,128)} %get-tuple-element.98), channel_id=1, source_target_pairs={{8,0},{12,4},{16,8},{20,12},{24,16},{28,20},{32,24},{36,28},{40,32... | collective-permute-start | bytes 6291464 | tf_op jit(solution)/shard_map/ppermute | solution.py:15
  645.4 254.3 %collective-permute-start.5 = (f32[256,2048]{1,0:T(8,128)}, f32[256,2048]{1,0:T(8,128)}, u32[]{:S(2)}, u32[]{:S(2)}) collective-permute-start(f32[256,2048]{1,0:T(8,128)} %get-tuple-element.96), channel_id=1, source_target_pairs={{12,0},{16,4},{20,8},{24,12},{28,16},{32,20},{36,24},{40,28},{44,3... | collective-permute-start | bytes 6291464 | tf_op jit(solution)/shard_map/ppermute | solution.py:15
  649.1 25.0 %collective-permute-start.4 = (f32[128,2048]{1,0:T(8,128)}, f32[128,2048]{1,0:T(8,128)}, u32[]{:S(2)}, u32[]{:S(2)}) collective-permute-start(f32[128,2048]{1,0:T(8,128)} %fusion.12), channel_id=1, source_target_pairs={{16,0},{20,4},{24,8},{28,12},{32,16},{36,20},{40,24},{44,28},{48,3... | collective-permute-start | bytes 3145736 | tf_op jit(solution)/shard_map/ppermute | solution.py:15
  (6 other events, 24.1 us)
Sparse Core Ops, SparseCore 0:
  30.1 196.1 reduce-scatter.9
  228.0 149.6 all-gather.2
  459.9 168.5 reduce-scatter.5
  630.1 265.3 all-gather.4
  897.9 222.7 reduce-scatter.7
where the time goes:
time: 1130 us
  waiting for transfers between devices  929 us (82%)
  local copies, waits for them, and re-layouts  66 us (6%)
  matrix products  60.4 us (5%)
  other arithmetic  36.3 us (3%)
  starting transfers between devices  21.2 us (2%)
  between operations  16 us (1%)
    all_gather x1, waiting for transfers between devices, local(): lax.all_gather(lax.psum_scatter(far_grad, 'seq', scatter_dimension=0, til...  219 us
    reduce_scatter x1, waiting for transfers between devices, local(): lax.psum_scatter(lax.dot_general(out_grad, attn_out.reshape(tok_dev, widt...  215 us
    reduce_scatter x1, waiting for transfers between devices, local(): lax.psum_scatter(far_mine, 'seq', scatter_dimension=0, tiled=True)  180 us
    reduce_scatter x1, waiting for transfers between devices, local(): lax.psum_scatter(far_grad, 'seq', scatter_dimension=0, tiled=True)  169 us
    all_gather x1, waiting for transfers between devices, local(): far_kv = lax.all_gather(far_part, 'seq', axis=0, tiled=True)  129 us
  transfers between devices with their start and end apart: 13, of which 6 were waited for; matrix products, arithmetic and copies ran while one was open for 5% of the time, Pallas kernels for 0%

commit v1 on v0

--- a/solution.py
+++ b/solution.py
@@ -56,7 +56,10 @@
         jnp.zeros_like(kv_blocks[:1]),
     ).reshape(summary_count * BLK, 2 * width)
     far_part = lax.psum_scatter(far_mine, "seq", scatter_dimension=0, tiled=True)
-    far_kv = lax.all_gather(far_part, "seq", axis=0, tiled=True)
+    size = lax.axis_size("seq")
+    parts = jnp.stack([far_part for _ in range(size)])
+    parts = lax.all_to_all(parts, "seq", split_axis=0, concat_axis=0)
+    far_kv = jnp.concatenate(parts, axis=0)
     all_kv = jnp.concatenate([pool_kv, far_kv], axis=0)
     key_rows = all_kv[:, :width].reshape(-1, heads_here, HD)
     value_rows = all_kv[:, width:].reshape(-1, heads_here, HD)

time: 1130 us -> 1000 us (0.88)
  waiting for transfers between devices: 929 us -> 794 us
    all_gather x1 -> x0, waiting for transfers between devices: 129 us -> none  [local(): far_kv = lax.all_gather(far_part, 'seq', axis=0, tiled=True)]
  transfers between devices with their start and end apart: 13 -> 13, of which waited for: 6 -> 6; matrix products, arithmetic and copies ran while one was open for 5% -> 6% of each run, Pallas kernels for 0% -> 0%
where the time goes in v1:
time: 1000 us
  waiting for transfers between devices  794 us (79%)
  local copies, waits for them, and re-layouts  69 us (7%)
  matrix products  62.4 us (6%)
  other arithmetic  33.4 us (3%)
  starting transfers between devices  26 us (3%)
  between operations  16 us (2%)
    all_gather x1, waiting for transfers between devices, local(): lax.all_gather(lax.psum_scatter(far_grad, 'seq', scatter_dimension=0, til...  214 us
    reduce_scatter x1, waiting for transfers between devices, local(): lax.psum_scatter(lax.dot_general(out_grad, attn_out.reshape(tok_dev, widt...  213 us
    reduce_scatter x1, waiting for transfers between devices, local(): lax.psum_scatter(far_mine, 'seq', scatter_dimension=0, tiled=True)  175 us
    reduce_scatter x1, waiting for transfers between devices, local(): lax.psum_scatter(far_grad, 'seq', scatter_dimension=0, tiled=True)  170 us
    ppermute x8, starting transfers between devices, passed_along(): return lax.ppermute(block, axis, route)  21 us
  transfers between devices with their start and end apart: 13, of which 6 were waited for; matrix products, arithmetic and copies ran while one was open for 6% of the time, Pallas kernels for 0%

profile of v1, /device:TPU:0, one launch (start us, length us, event | category | flops | bytes accessed | tf_op | source)
XLA Modules:
  0.0 1000.4 jit_solution(1577455977665321503)
XLA Ops:
  18.2 6.0 collective-permute-start.1
  24.2 4.9 collective-permute-start.2
  35.7 6.5 convolution_convert_fusion.2
  42.5 174.8 %reduce-scatter.4.cloned.1.call-done = bf16[16,2048]{1,0:T(8,128)(2,1)} async-done(((bf16[512,2048]{1,0:T(8,128)(2,1)}), bf16[16,2048]{1,0:T(8,128)(2,1)}) %reduce-scatter.4.cloned.1.call-update) | async-done | bytes 65552 | tf_op jit(solution)/shard_map/reduce_scatter | solution.py:58
  219.7 4.8 all-to-all-start
  246.0 6.7 fusion.23
  252.7 5.9 copy.89
  258.5 5.6 copy.95
  264.1 9.4 fusion.1
  273.5 7.8 exponential_reduce_fusion
  281.3 10.4 %multiply_reduce_fusion = (f32[256,8]{0,1:T(8,128)S(1)}, bf16[8,128,256]{2,1,0:T(8,128)(2,1)}) fusion(bf16[256,1024]{0,1:T(8,128)(2,1)} %copy.118, bf16[1664,8,128]{0,2,1:T(8,128)(2,1)} %bitcast.94, f32[8,1664,256]{2,1,0:T(8,128)} %get-tuple-element.105, f32[8,256]{1,0:T(8,128)S(1)} %log_add_fusion, pred[256,1664]{0,1:T(8,128)(4,1)S(1)} %copy-done.2), kind=kOutput, calls=%fused_computation.41 | convolution fusion | flops 887355392 | bytes 18530304 | tf_op jit(solution)/shard_map/hqk,khd->qhd/dot_general | solution.py:97
  291.8 5.8 fusion.20
  297.6 10.1 %multiply_convert_fusion = bf16[8,256,1664]{1,2,0:T(8,128)(2,1)} fusion(f32[8,1664,256]{2,1,0:T(8,128)S(1)} %bitcast.86, f32[8,256]{1,0:T(8,128)S(1)} %bitcast.103, f32[8,256]{1,0:T(8,128)S(1)} %log_add_fusion, pred[256,1664]{0,1:T(8,128)(4,1)S(1)} %copy-done.2, bf16[256,8,128]{0,2,1:T(8,128)(2,1)} %bitcast.97, bf16[1664,8,128]{0,2,1:T(8,128)(2,1)} %bitcast.95), kind=kOutput, calls=%fused_computation.15 | convolution fusion | flops 896270336 | bytes 24821760 | tf_op jit(solution)/shard_map/qhd,khd->hqk/dot_general | solution.py:103
  307.7 7.7 copy.107
  315.4 7.9 fusion.25
  323.3 7.7 copy.106
  331.0 4.7 pad_maximum_fusion
  335.8 169.5 %reduce-scatter.6.cloned.1.call-done = f32[16,2048]{1,0:T(8,128)} async-done(((f32[512,2048]{1,0:T(8,128)}), f32[16,2048]{1,0:T(8,128)}) %reduce-scatter.6.cloned.1.call-update) | async-done | bytes 131088 | tf_op jit(solution)/shard_map/reduce_scatter | solution.py:115
  505.4 8.1 convolution_bitcast_fusion
  513.5 6.1 fusion.4
  532.4 19.3 %collective-permute-done.4 = f32[128,2048]{1,0:T(8,128)} collective-permute-done((f32[128,2048]{1,0:T(8,128)}, f32[128,2048]{1,0:T(8,128)}, u32[]{:S(2)}, u32[]{:S(2)}) %collective-permute-start.4) | collective-permute-done | bytes 1048608 | tf_op jit(solution)/shard_map/ppermute | solution.py:15
  554.4 214.2 %all-gather.2.cloned.1.call-done = f32[512,2048]{1,0:T(8,128)} async-done(((f32[16,2048]{1,0:T(8,128)}), f32[512,2048]{1,0:T(8,128)}) %all-gather.2.cloned.1.call-update) | async-done | bytes 4194320 | tf_op jit(solution)/shard_map/all_gather | solution.py:114
  772.8 4.6 fusion.8
  778.5 213.4 %reduce-scatter.8.cloned.1.call-done = f32[128,1024]{0,1:T(8,128)} async-done(((f32[4096,1024]{0,1:T(8,128)}), f32[128,1024]{0,1:T(8,128)}) %reduce-scatter.8.cloned.1.call-update) | async-done | bytes 524304 | tf_op jit(solution)/shard_map/reduce_scatter | solution.py:132
  (105 shorter events, 62.5 us)
Async XLA Ops:
  7.2 28.6 %copy-start = (bf16[256,4096]{1,0:T(8,128)(2,1)S(1)}, bf16[256,4096]{1,0:T(8,128)(2,1)}, u32[]{:S(2)}) copy-start(bf16[256,4096]{1,0:T(8,128)(2,1)} %param.23) | copy-start | bytes 6291460
  7.2 210.1 %reduce-scatter.4.cloned.1.call-start = ((), (), s32[]{:S(2)}) async-start(), calls=%async_computation.4 | async-start | bytes 2162688 | tf_op jit(solution)/shard_map/reduce_scatter | solution.py:58
  10.6 24.4 %copy-start.9 = (s32[64,12]{0,1:T(8,128)S(1)}, s32[64,12]{0,1:T(8,128)}, u32[]{:S(2)}) copy-start(s32[64,12]{0,1:T(8,128)} %param.25) | copy-start | bytes 9220
  18.2 213.6 %collective-permute-start.1 = (bf16[256,2048]{1,0:T(8,128)(2,1)S(1)}, bf16[256,2048]{1,0:T(8,128)(2,1)}, u32[]{:S(2)}, u32[]{:S(2)}) collective-permute-start(bf16[256,2048]{1,0:T(8,128)(2,1)S(1)} %constant_dynamic-update-slice_fusion), channel_id=1, source_target_pairs={{0,12},{4,16},{8,20},{12,24},{16,28},{20,32},{24,36},{28,40},{32,4... | collective-permute-start | bytes 3145736 | tf_op jit(solution)/shard_map/ppermute | solution.py:15
  24.2 209.9 %collective-permute-start.2 = (bf16[256,2048]{1,0:T(8,128)(2,1)S(1)}, bf16[256,2048]{1,0:T(8,128)(2,1)}, u32[]{:S(2)}, u32[]{:S(2)}) collective-permute-start(bf16[256,2048]{1,0:T(8,128)(2,1)S(1)} %constant_dynamic-update-slice_fusion), channel_id=1, source_target_pairs={{0,8},{4,12},{8,16},{12,20},{16,24},{20,28},{24,32},{28,36},{32,40... | collective-permute-start | bytes 3145736 | tf_op jit(solution)/shard_map/ppermute | solution.py:15
  29.2 207.3 %collective-permute-start.3 = (bf16[256,2048]{1,0:T(8,128)(2,1)S(1)}, bf16[256,2048]{1,0:T(8,128)(2,1)}, u32[]{:S(2)}, u32[]{:S(2)}) collective-permute-start(bf16[256,2048]{1,0:T(8,128)(2,1)S(1)} %constant_dynamic-update-slice_fusion), channel_id=1, source_target_pairs={{0,4},{4,8},{8,12},{12,16},{16,20},{20,24},{24,28},{28,32},{32,36}... | collective-permute-start | bytes 3145736 | tf_op jit(solution)/shard_map/ppermute | solution.py:15
  32.9 197.1 %collective-permute-start = (bf16[128,2048]{1,0:T(8,128)(2,1)}, bf16[128,2048]{1,0:T(8,128)(2,1)}, u32[]{:S(2)}, u32[]{:S(2)}) collective-permute-start(bf16[128,2048]{1,0:T(8,128)(2,1)} %slice.115), channel_id=1, source_target_pairs={{0,16},{4,20},{8,24},{12,28},{16,32},{20,36},{24,40},{28,44},{32,4... | collective-permute-start | bytes 1572872 | tf_op jit(solution)/shard_map/ppermute | solution.py:15
  219.7 23.1 %all-to-all-start = ((bf16[32,16,2048]{2,1,0:T(8,128)(2,1)}), bf16[32,16,2048]{2,1,0:T(8,128)(2,1)}, u32[]{:S(2)}, u32[]{:S(2)}) async-start(bf16[32,16,2048]{2,1,0:T(8,128)(2,1)} %stack.2), calls=%async_computation.1 | async-start | bytes 4194304 | tf_op jit(solution)/shard_map/all_to_all | solution.py:61
  224.5 280.8 %reduce-scatter.6.cloned.1.call-start = ((), (), s32[]{:S(2)}) async-start(), calls=%async_computation.5 | async-start | bytes 4325376 | tf_op jit(solution)/shard_map/reduce_scatter | solution.py:115
  228.7 10.9 %copy-start.7 = (bf16[256,1024]{1,0:T(8,128)(2,1)S(1)}, bf16[256,1024]{1,0:T(8,128)(2,1)}, u32[]{:S(2)}) copy-start(bf16[256,1024]{1,0:T(8,128)(2,1)} %param.22) | copy-start | bytes 1572868
  252.7 11.4 %copy-start.2 = (pred[256,1664]{0,1:T(8,128)(4,1)S(1)}, pred[256,1664]{0,1:T(8,128)(4,1)}, u32[]{:S(2)}) copy-start(pred[256,1664]{0,1:T(8,128)(4,1)} %bitcast_and_fusion) | copy-start | bytes 1277956
  252.7 11.4 %copy-start.3 = (bf16[256,1024]{0,1:T(8,128)(2,1)S(1)}, bf16[256,1024]{0,1:T(8,128)(2,1)}, u32[]{:S(2)}) copy-start(bf16[256,1024]{0,1:T(8,128)(2,1)} %copy.117) | copy-start | bytes 1572868
  273.5 18.2 %slice-start = ((s8[13631488]{0:T(1024)(128)(4,1)}), s8[4194304]{0:T(1024)(128)(4,1)S(1)}, s32[]{:S(2)}) async-start(s8[13631488]{0:T(1024)(128)(4,1)} %bitcast.85), calls=%async_computation.8 | async-start | bytes 8388608
  273.5 18.2 %slice-start.1 = ((s8[13631488]{0:T(1024)(128)(4,1)}), s8[1048576]{0:T(1024)(128)(4,1)S(1)}, s32[]{:S(2)}) async-start(s8[13631488]{0:T(1024)(128)(4,1)} %bitcast.85), calls=%async_computation.9 | async-start | bytes 2097152
  281.3 10.4 %slice-start.2 = ((s8[13631488]{0:T(1024)(128)(4,1)}), s8[4194304]{0:T(1024)(128)(4,1)S(1)}, s32[]{:S(2)}) async-start(s8[13631488]{0:T(1024)(128)(4,1)} %bitcast.85), calls=%async_computation.10 | async-start | bytes 8388608
  281.3 10.4 %slice-start.3 = ((s8[13631488]{0:T(1024)(128)(4,1)}), s8[4194304]{0:T(1024)(128)(4,1)S(1)}, s32[]{:S(2)}) async-start(s8[13631488]{0:T(1024)(128)(4,1)} %bitcast.85), calls=%async_computation.11 | async-start | bytes 8388608
  281.3 10.4 %copy-start.5 = (bf16[256,1024]{0,1:T(8,128)(2,1)S(1)}, bf16[256,1024]{0,1:T(8,128)(2,1)}, u32[]{:S(2)}) copy-start(bf16[256,1024]{0,1:T(8,128)(2,1)} %copy.118) | copy-start | bytes 1572868
  331.0 174.4 %copy-start.8 = (bf16[8,128,256]{2,1,0:T(8,128)(2,1)S(1)}, bf16[8,128,256]{2,1,0:T(8,128)(2,1)}, u32[]{:S(2)}) copy-start(bf16[8,128,256]{2,1,0:T(8,128)(2,1)} %get-tuple-element.107) | copy-start | bytes 1572868
  335.7 432.8 %all-gather.2.cloned.1.call-start = ((), (), s32[]{:S(2)}) async-start(), calls=%async_computation.6 | async-start | bytes 4325376 | tf_op jit(solution)/shard_map/all_gather | solution.py:114
  505.4 486.5 %reduce-scatter.8.cloned.1.call-start = ((), (), s32[]{:S(2)}) async-start(), calls=%async_computation.7 | async-start | bytes 17301504 | tf_op jit(solution)/shard_map/reduce_scatter | solution.py:132
  519.6 253.2 %collective-permute-start.7 = (f32[256,2048]{1,0:T(8,128)}, f32[256,2048]{1,0:T(8,128)}, u32[]{:S(2)}, u32[]{:S(2)}) collective-permute-start(f32[256,2048]{1,0:T(8,128)} %get-tuple-element.99), channel_id=1, source_target_pairs={{4,0},{8,4},{12,8},{16,12},{20,16},{24,20},{28,24},{32,28},{36,32}... | collective-permute-start | bytes 6291464 | tf_op jit(solution)/shard_map/ppermute | solution.py:15
  520.9 251.9 %collective-permute-start.6 = (f32[256,2048]{1,0:T(8,128)}, f32[256,2048]{1,0:T(8,128)}, u32[]{:S(2)}, u32[]{:S(2)}) collective-permute-start(f32[256,2048]{1,0:T(8,128)} %get-tuple-element.98), channel_id=1, source_target_pairs={{8,0},{12,4},{16,8},{20,12},{24,16},{28,20},{32,24},{36,28},{40,32... | collective-permute-start | bytes 6291464 | tf_op jit(solution)/shard_map/ppermute | solution.py:15
  522.2 250.6 %collective-permute-start.5 = (f32[256,2048]{1,0:T(8,128)}, f32[256,2048]{1,0:T(8,128)}, u32[]{:S(2)}, u32[]{:S(2)}) collective-permute-start(f32[256,2048]{1,0:T(8,128)} %get-tuple-element.96), channel_id=1, source_target_pairs={{12,0},{16,4},{20,8},{24,12},{28,16},{32,20},{36,24},{40,28},{44,3... | collective-permute-start | bytes 6291464 | tf_op jit(solution)/shard_map/ppermute | solution.py:15
  525.9 25.9 %collective-permute-start.4 = (f32[128,2048]{1,0:T(8,128)}, f32[128,2048]{1,0:T(8,128)}, u32[]{:S(2)}, u32[]{:S(2)}) collective-permute-start(f32[128,2048]{1,0:T(8,128)} %fusion.13), channel_id=1, source_target_pairs={{16,0},{20,4},{24,8},{28,12},{32,16},{36,20},{40,24},{44,28},{48,3... | collective-permute-start | bytes 3145736 | tf_op jit(solution)/shard_map/ppermute | solution.py:15
  (3 other events, 21.6 us)
Sparse Core Ops, SparseCore 0:
  18.4 198.8 reduce-scatter.3
  335.9 169.4 reduce-scatter.5
  507.1 261.4 all-gather.1
  770.9 220.8 reduce-scatter.7
